TPU v7x, 32 devices: a whole 2x2x4 slice. The times are simulated.
32 devices in a mesh: mode: 2 (over y), col: 16 (over z, x, core).
Axes of the slice: x: 2, y: 2, z: 4, core: 2. Of those that a mesh axis runs over, the one named last changes fastest.
Arguments:
- tensor: float32 [512, 16, 4096], P('mode', 'col'), may hold values from -15 to 15
- start_basis: float32 [512, 128], replicated, may hold values from -6 to 6
Outputs:
- factor: float32 [512, 512], replicated
- basis: float32 [512, 128], replicated
- core: float32 [128, 16, 4096], P(None, 'col', 'mode')
All inputs are finite; a program needn't handle non-finite values.
Results may differ from a plain program's by a relative error of at most 0.00018.
Values sent between devices are 32-bit elements; how exact they have to be, the bound alone decides.
A program may use at most 64 MiB of HBM per device.

v0:
```python
import jax
import jax.numpy as jnp
from jax import lax
from jax.sharding import PartitionSpec as P

POWER = 2


def matmul(left, right):
    return jnp.dot(left, right, precision=lax.Precision.HIGHEST, preferred_element_type=jnp.float32)


def orthonormal(image):
    small = jnp.linalg.cholesky(matmul(image.T, image))
    return jax.scipy.linalg.solve_triangular(small, image.T, lower=True).T


def per_device(tensor, start_basis):
    regrouped = lax.all_to_all(tensor, "mode", split_axis=2, concat_axis=0, tiled=True)
    rows = regrouped.shape[0]
    flat = regrouped.reshape(rows, -1)
    columns = flat.shape[1] * lax.axis_size("mode") * lax.axis_size("col")
    gram = matmul(flat, flat.T)
    total = lax.psum(gram, ("mode", "col"))
    factor = jnp.linalg.cholesky(total / columns)
    basis = start_basis
    for step in range(POWER):
        image = matmul(factor, matmul(factor.T, basis))
        basis = orthonormal(image)
    core = matmul(basis.T, flat).reshape(basis.shape[1], regrouped.shape[1], regrouped.shape[2])
    return (factor, basis, core)


def solution(mesh):
    in_specs = (P("mode", "col", None), P())
    out_specs = (P(), P(), P(None, "col", "mode"))
    return jax.shard_map(
        per_device, mesh=mesh, in_specs=in_specs, out_specs=out_specs, check_vma=False
    )
```

profile of v0, /device:TPU:0, one launch (start us, length us, event | category | flops | bytes accessed | tf_op | source)
XLA Modules:
  0.0 377.8 jit_solution(11997995047091231864)
XLA Ops:
  7.2 14.3 %copy.25 = f32[256,1,4096]{0,1,2:T(1,128)} copy(f32[256,1,4096]{2,1,0:T(1,128)} %param.5) | data formatting | bytes 8388608 | tf_op args[0]
  21.5 52.9 %all_to_all.15 = f32[256,1,4096]{0,1,2:T(1,128)S(1)} all-to-all(f32[256,1,4096]{0,1,2:T(1,128)} %copy.25), channel_id=1, replica_groups=mesh['mode'=2,'col'=16] {'mode'}, dimensions={2} | all-to-all | bytes 8388608 | tf_op jit(solution)/shard_map/all_to_all | solution.py:19
  74.4 2.2 copy.34
  76.7 5.4 %copy.26 = f32[2,256,1,2048]{3,1,0,2:T(8,128)} copy(f32[2,256,1,2048]{1,3,0,2:T(8,128)} %bitcast.71) | data formatting | bytes 8388608 | tf_op jit(solution)/shard_map/all_to_all | solution.py:19
  82.1 10.3 %fusion.22 = f32[512,512]{0,1:T(8,128)} fusion(f32[512,2048]{1,0:T(8,128)} %bitcast.69), kind=kOutput, calls=%fused_computation.57 | convolution fusion | flops 6442450944 | bytes 5242880 | tf_op jit(solution)/shard_map/dot_general | solution.py:10
  92.4 131.3 %all-reduce.3.cloned.1.call-done = f32[512,512]{0,1:T(8,128)} async-done(((f32[512,512]{0,1:T(8,128)}), f32[512,512]{0,1:T(8,128)}) %all-reduce.3.cloned.1.call-update) | async-done | bytes 1048592 | tf_op jit(solution)/shard_map/psum | solution.py:24
  223.8 1.4 broadcast_multiply_fusion
  225.2 0.3 copy.28
  225.5 0.2 fusion
  225.8 11.7 %cholesky.120 = f32[128,128]{1,0:T(8,128)S(1)} custom-call(f32[128,128]{1,0:T(8,128)S(1)} %cholesky.330), custom_call_target="Cholesky" | custom-call | tf_op jit(solution)/shard_map/jit(cholesky)/cholesky | solution.py:25
  237.5 9.8 %custom-call.32 = f32[1,128,128]{1,2,0:T(8,128)S(1)} custom-call(f32[1,128,128]{2,1,0:T(8,128)S(1)} %get-tuple-element.26), custom_call_target="InvertDiagBlocksLowerTriangular" | custom-call | tf_op jit(solution)/shard_map/jit(cholesky)/cholesky | solution.py:25
  247.4 0.1 cholesky.251
  247.5 0.3 constant_dynamic-update-slice_fusion.2
  247.8 0.3 convolution_subtract_fusion
  248.2 11.7 %cholesky.244 = f32[128,128]{1,0:T(8,128)S(1)} custom-call(f32[128,128]{1,0:T(8,128)S(1)} %cholesky.334), custom_call_target="Cholesky" | custom-call | tf_op jit(solution)/shard_map/jit(cholesky)/cholesky | solution.py:25
  259.9 10.0 %custom-call.33 = f32[1,128,128]{1,2,0:T(8,128)S(1)} custom-call(f32[1,128,128]{2,1,0:T(8,128)S(1)} %get-tuple-element.23), custom_call_target="InvertDiagBlocksLowerTriangular" | custom-call | tf_op jit(solution)/shard_map/jit(cholesky)/cholesky | solution.py:25
  269.9 0.3 convolution_dynamic-update-slice_fusion
  270.2 0.4 convolution_subtract_fusion.1
  270.6 11.7 %cholesky.265 = f32[128,128]{1,0:T(8,128)S(1)} custom-call(f32[128,128]{1,0:T(8,128)S(1)} %cholesky.339), custom_call_target="Cholesky" | custom-call | tf_op jit(solution)/shard_map/jit(cholesky)/cholesky | solution.py:25
  282.3 0.6 compare_reduce_fusion.3
  283.0 9.8 %custom-call.34 = f32[1,128,128]{1,2,0:T(8,128)S(1)} custom-call(f32[1,128,128]{2,1,0:T(8,128)S(1)} %get-tuple-element.20), custom_call_target="InvertDiagBlocksLowerTriangular" | custom-call | tf_op jit(solution)/shard_map/jit(cholesky)/cholesky | solution.py:25
  292.8 0.2 convolution_dynamic-update-slice_fusion.1
  293.0 0.4 convolution_subtract_fusion.2
  293.4 11.7 %cholesky.282 = f32[128,128]{1,0:T(8,128)S(1)} custom-call(f32[128,128]{1,0:T(8,128)S(1)} %convolution_subtract_fusion.2), custom_call_target="Cholesky" | custom-call | tf_op jit(solution)/shard_map/jit(cholesky)/cholesky | solution.py:25
  305.1 0.7 compare_reduce_fusion.2
  305.8 0.6 compare_reduce_fusion.4
  309.4 0.1 select_select_fusion
  309.5 1.8 fusion.23
  311.3 1.0 fusion.24
  312.3 0.6 fusion.25
  312.9 0.1 copy.29
  313.0 11.7 %cholesky.310 = f32[128,128]{1,0:T(8,128)S(1)} custom-call(f32[128,128]{1,0:T(8,128)S(1)} %fusion.18), custom_call_target="Cholesky" | custom-call | tf_op jit(solution)/shard_map/jit(cholesky)/cholesky | solution.py:14
  324.8 0.6 compare_reduce_fusion.1
  325.4 0.7 fusion.11
  326.1 9.8 %custom-call.36 = f32[1,128,128]{1,2,0:T(8,128)S(1)} custom-call(f32[1,128,128]{2,1,0:T(8,128)S(1)} %fusion.11), custom_call_target="InvertDiagBlocksLowerTriangular" | custom-call | tf_op jit(solution)/shard_map/jit(_solve_triangular)/triangular_solve | solution.py:15
  335.9 0.4 fusion.4
  336.3 1.8 fusion.26
  338.1 1.2 fusion.27
  339.3 0.6 fusion.28
  339.9 0.1 copy.30
  340.0 11.7 %cholesky.321 = f32[128,128]{1,0:T(8,128)S(1)} custom-call(f32[128,128]{1,0:T(8,128)S(1)} %fusion.16), custom_call_target="Cholesky" | custom-call | tf_op jit(solution)/shard_map/jit(cholesky)/cholesky | solution.py:14
  351.8 0.6 compare_reduce_fusion
  352.4 0.7 fusion.12
  353.1 9.8 %custom-call.37 = f32[1,128,128]{1,2,0:T(8,128)S(1)} custom-call(f32[1,128,128]{2,1,0:T(8,128)S(1)} %fusion.12), custom_call_target="InvertDiagBlocksLowerTriangular" | custom-call | tf_op jit(solution)/shard_map/jit(_solve_triangular)/triangular_solve | solution.py:15
  362.9 0.4 fusion.2
  363.3 4.6 %convolution_bitcast_fusion = f32[128,1,2048]{2,0,1:T(8,128)S(1)} fusion(f32[128,512]{1,0:T(8,128)S(1)} %fusion.2, f32[512,2048]{1,0:T(8,128)} %bitcast.70), kind=kOutput, calls=%fused_computation | convolution fusion | flops 1610612736 | bytes 5505024 | tf_op jit(solution)/shard_map/dot_general | solution.py:10
  367.9 2.0 copy.32
  369.9 0.8 copy.31
  (19 shorter events, 0.3 us)
Async XLA Ops:
  7.2 302.3 %copy-start = (f32[512,128]{1,0:T(8,128)S(1)}, f32[512,128]{1,0:T(8,128)}, u32[]{:S(2)}) copy-start(f32[512,128]{1,0:T(8,128)} %param.6) | copy-start | bytes 786436
  7.2 216.6 %all-reduce.3.cloned.1.call-start = ((), (), s32[]{:S(2)}) async-start(), calls=%async_computation.1 | async-start | bytes 2097152 | tf_op jit(solution)/shard_map/psum | solution.py:24
  223.8 1.8 copy-start.2
  309.5 30.4 %copy-start.1 = (f32[512,512]{1,0:T(8,128)}, f32[512,512]{1,0:T(8,128)S(1)}, u32[]{:S(2)}) copy-start(f32[512,512]{1,0:T(8,128)S(1)} %select_select_fusion) | copy-start | bytes 3145732
Sparse Core Ops, SparseCore 0:
  92.6 131.1 all-reduce.2
where the time goes:
time: 382 us; the launch traced here: 378 us
  waiting for transfers between devices  131 us (34%)
  other arithmetic  126 us (33%)
  blocking collectives  52.9 us (14%)
  local copies, waits for them, and re-layouts  25.4 us (7%)
  matrix products  24.6 us (6%)
  between operations  17.5 us (5%)
    psum x1, waiting for transfers between devices, per_device(): total = lax.psum(gram, ('mode', 'col'))  131 us
    another operation x14, other arithmetic, per_device(): factor = jnp.linalg.cholesky(total / columns)  78.5 us
    all_to_all x1, blocking collectives, per_device(): lax.all_to_all(tensor, 'mode', split_axis=2, concat_axis=0, tiled=True)  52.9 us
    another operation x6, other arithmetic, orthonormal(): small = jnp.linalg.cholesky(matmul(image.T, image))  24.8 us
    dot_general x8, matrix products, matmul(): jnp.dot(left, right, precision=lax.Precision.HIGHEST, preferred_element_t...  21.9 us
    another operation x4, other arithmetic, orthonormal(): return jax.scipy.linalg.solve_triangular(small, image.T, lower=True).T  20.9 us
    unnamed x10, local copies, waits for them, and re-layouts  19.4 us
  transfers between devices with their start and end apart: 1, of which 1 were waited for; matrix products, arithmetic and copies ran while one was open for 0% of the time, Pallas kernels for 0%

commit v1 on v0

--- a/solution.py
+++ b/solution.py
@@ -1,9 +1,18 @@
+import functools
 import jax
 import jax.numpy as jnp
 from jax import lax
 from jax.sharding import PartitionSpec as P
+from jax.lax import all_gather
 
 POWER = 2
+
+
+def resolve_matrix_for(s0, along_axis):
+    return jnp.sum(all_gather(s0, along_axis), 0)
+
+
+cover_the_sheets = functools.partial(resolve_matrix_for, along_axis=("mode", "col"))
 
 
 def matmul(left, right):
@@ -21,7 +30,7 @@
     flat = regrouped.reshape(rows, -1)
     columns = flat.shape[1] * lax.axis_size("mode") * lax.axis_size("col")
     gram = matmul(flat, flat.T)
-    total = lax.psum(gram, ("mode", "col"))
+    total = cover_the_sheets(gram)
     factor = jnp.linalg.cholesky(total / columns)
     basis = start_basis
     for step in range(POWER):

time: 382 us -> 457 us (1.20)
  waiting for transfers between devices: 131 us -> 195 us
  other arithmetic: 126 us -> 137 us
    all_gather x0 -> x1, waiting for transfers between devices: none -> 195 us  [resolve_matrix_for(): return jnp.sum(all_gather(s0, along_axis), 0)]
    psum x1 -> x0, waiting for transfers between devices: 131 us -> none  [per_device(): total = lax.psum(gram, ('mode', 'col'))]
    reduce_sum x0 -> x1, other arithmetic: none -> 12.4 us  [resolve_matrix_for(): return jnp.sum(all_gather(s0, along_axis), 0)]
    unnamed x10 -> x8, local copies, waits for them, and re-layouts: 19.4 us -> 19.4 us
where the time goes in v1:
time: 457 us; the launch traced here: 452 us
  waiting for transfers between devices  195 us (43%)
  other arithmetic  137 us (30%)
  blocking collectives  52.9 us (12%)
  local copies, waits for them, and re-layouts  25.4 us (6%)
  matrix products  24.9 us (5%)
  between operations  17.1 us (4%)
    all_gather x1, waiting for transfers between devices, resolve_matrix_for(): return jnp.sum(all_gather(s0, along_axis), 0)  195 us
    another operation x14, other arithmetic, per_device(): factor = jnp.linalg.cholesky(total / columns)  78.6 us
    all_to_all x1, blocking collectives, per_device(): lax.all_to_all(tensor, 'mode', split_axis=2, concat_axis=0, tiled=True)  52.9 us
    another operation x6, other arithmetic, orthonormal(): small = jnp.linalg.cholesky(matmul(image.T, image))  24.8 us
    dot_general x8, matrix products, matmul(): jnp.dot(left, right, precision=lax.Precision.HIGHEST, preferred_element_t...  22.2 us
    another operation x4, other arithmetic, orthonormal(): return jax.scipy.linalg.solve_triangular(small, image.T, lower=True).T  20.9 us
    unnamed x8, local copies, waits for them, and re-layouts  19.4 us
    reduce_sum x1, other arithmetic, resolve_matrix_for(): return jnp.sum(all_gather(s0, along_axis), 0)  12.4 us
  transfers between devices with their start and end apart: 1, of which 1 were waited for; matrix products, arithmetic and copies ran while one was open for 0% of the time, Pallas kernels for 0%

profile of v1, /device:TPU:0, one launch (start us, length us, event | category | flops | bytes accessed | tf_op | source)
XLA Modules:
  0.0 452.4 jit_solution(16015458273392011050)
XLA Ops:
  7.2 14.3 %copy.22 = f32[256,1,4096]{0,1,2:T(1,128)} copy(f32[256,1,4096]{2,1,0:T(1,128)} %param.5) | data formatting | bytes 8388608 | tf_op args[0]
  21.5 52.9 %all_to_all.15 = f32[256,1,4096]{0,1,2:T(1,128)S(1)} all-to-all(f32[256,1,4096]{0,1,2:T(1,128)} %copy.22), channel_id=1, replica_groups=mesh['mode'=2,'col'=16] {'mode'}, dimensions={2} | all-to-all | bytes 8388608 | tf_op jit(solution)/shard_map/all_to_all | solution.py:28
  74.4 2.2 copy.29
  76.6 5.4 %copy.23 = f32[2,256,1,2048]{3,1,0,2:T(8,128)} copy(f32[2,256,1,2048]{1,3,0,2:T(8,128)} %bitcast.73) | data formatting | bytes 8388608 | tf_op jit(solution)/shard_map/all_to_all | solution.py:28
  82.0 10.3 %fusion.22 = f32[512,512]{1,0:T(8,128)} fusion(f32[512,2048]{1,0:T(8,128)} %bitcast.70), kind=kOutput, calls=%fused_computation.56 | convolution fusion | flops 6442450944 | bytes 5242880 | tf_op jit(solution)/shard_map/dot_general | solution.py:19
  92.3 194.9 %all-gather.3.cloned.1.call-done = f32[16384,512]{1,0:T(8,128)} async-done(((f32[512,512]{1,0:T(8,128)}), f32[16384,512]{1,0:T(8,128)}) %all-gather.3.cloned.1.call-update) | async-done | bytes 33554448 | tf_op jit(solution)/shard_map/all_gather | solution.py:12
  287.2 12.4 %reduce_sum.11 = f32[512,512]{1,0:T(8,128)S(1)} reduce(f32[32,512,512]{2,1,0:T(8,128)} %bitcast.72, f32[]{:T(128)} %constant.164.clone.1), dimensions={0}, to_apply=%region_0.0 | reduce | flops 8126464 | bytes 34603012 | tf_op jit(solution)/shard_map/reduce_sum | solution.py:12
  299.6 0.3 copy.24
  300.0 0.2 fusion
  300.2 11.7 %cholesky.120 = f32[128,128]{1,0:T(8,128)S(1)} custom-call(f32[128,128]{1,0:T(8,128)S(1)} %cholesky.330), custom_call_target="Cholesky" | custom-call | tf_op jit(solution)/shard_map/jit(cholesky)/cholesky | solution.py:34
  312.0 0.1 cholesky.251
  312.1 9.8 %custom-call.32 = f32[1,128,128]{1,2,0:T(8,128)S(1)} custom-call(f32[1,128,128]{2,1,0:T(8,128)S(1)} %get-tuple-element.26), custom_call_target="InvertDiagBlocksLowerTriangular" | custom-call | tf_op jit(solution)/shard_map/jit(cholesky)/cholesky | solution.py:34
  321.9 0.3 constant_dynamic-update-slice_fusion.2
  322.2 0.3 convolution_subtract_fusion
  322.6 11.7 %cholesky.244 = f32[128,128]{1,0:T(8,128)S(1)} custom-call(f32[128,128]{1,0:T(8,128)S(1)} %cholesky.334), custom_call_target="Cholesky" | custom-call | tf_op jit(solution)/shard_map/jit(cholesky)/cholesky | solution.py:34
  334.3 10.0 %custom-call.33 = f32[1,128,128]{1,2,0:T(8,128)S(1)} custom-call(f32[1,128,128]{2,1,0:T(8,128)S(1)} %get-tuple-element.23), custom_call_target="InvertDiagBlocksLowerTriangular" | custom-call | tf_op jit(solution)/shard_map/jit(cholesky)/cholesky | solution.py:34
  344.3 0.3 convolution_dynamic-update-slice_fusion
  344.6 0.4 convolution_subtract_fusion.1
  345.0 11.7 %cholesky.265 = f32[128,128]{1,0:T(8,128)S(1)} custom-call(f32[128,128]{1,0:T(8,128)S(1)} %cholesky.339), custom_call_target="Cholesky" | custom-call | tf_op jit(solution)/shard_map/jit(cholesky)/cholesky | solution.py:34
  356.8 0.6 compare_reduce_fusion.3
  357.4 9.8 %custom-call.34 = f32[1,128,128]{1,2,0:T(8,128)S(1)} custom-call(f32[1,128,128]{2,1,0:T(8,128)S(1)} %get-tuple-element.20), custom_call_target="InvertDiagBlocksLowerTriangular" | custom-call | tf_op jit(solution)/shard_map/jit(cholesky)/cholesky | solution.py:34
  367.2 0.2 convolution_dynamic-update-slice_fusion.1
  367.4 0.4 convolution_subtract_fusion.2
  367.8 11.7 %cholesky.282 = f32[128,128]{1,0:T(8,128)S(1)} custom-call(f32[128,128]{1,0:T(8,128)S(1)} %convolution_subtract_fusion.2), custom_call_target="Cholesky" | custom-call | tf_op jit(solution)/shard_map/jit(cholesky)/cholesky | solution.py:34
  379.6 0.7 compare_reduce_fusion.2
  380.3 0.6 compare_reduce_fusion.4
  383.6 0.1 select_select_fusion
  383.7 2.2 fusion.23
  385.9 1.0 fusion.24
  386.9 0.6 fusion.25
  387.5 0.1 copy.25
  387.6 11.7 %cholesky.310 = f32[128,128]{1,0:T(8,128)S(1)} custom-call(f32[128,128]{1,0:T(8,128)S(1)} %fusion.18), custom_call_target="Cholesky" | custom-call | tf_op jit(solution)/shard_map/jit(cholesky)/cholesky | solution.py:23
  399.4 0.6 compare_reduce_fusion.1
  400.0 0.7 fusion.11
  400.7 9.8 %custom-call.36 = f32[1,128,128]{1,2,0:T(8,128)S(1)} custom-call(f32[1,128,128]{2,1,0:T(8,128)S(1)} %fusion.11), custom_call_target="InvertDiagBlocksLowerTriangular" | custom-call | tf_op jit(solution)/shard_map/jit(_solve_triangular)/triangular_solve | solution.py:24
  410.5 0.4 fusion.4
  410.9 1.8 fusion.26
  412.7 1.2 fusion.27
  413.9 0.6 fusion.28
  414.5 0.1 copy.26
  414.6 11.7 %cholesky.321 = f32[128,128]{1,0:T(8,128)S(1)} custom-call(f32[128,128]{1,0:T(8,128)S(1)} %fusion.16), custom_call_target="Cholesky" | custom-call | tf_op jit(solution)/shard_map/jit(cholesky)/cholesky | solution.py:23
  426.4 0.6 compare_reduce_fusion
  427.0 0.7 fusion.12
  427.7 9.8 %custom-call.37 = f32[1,128,128]{1,2,0:T(8,128)S(1)} custom-call(f32[1,128,128]{2,1,0:T(8,128)S(1)} %fusion.12), custom_call_target="InvertDiagBlocksLowerTriangular" | custom-call | tf_op jit(solution)/shard_map/jit(_solve_triangular)/triangular_solve | solution.py:24
  437.5 0.4 fusion.2
  437.9 4.5 %convolution_bitcast_fusion = f32[128,1,2048]{2,0,1:T(8,128)S(1)} fusion(f32[128,512]{1,0:T(8,128)S(1)} %fusion.2, f32[512,2048]{1,0:T(8,128)} %bitcast.71), kind=kOutput, calls=%fused_computation | convolution fusion | flops 1610612736 | bytes 5505024 | tf_op jit(solution)/shard_map/dot_general | solution.py:19
  442.5 2.0 copy.28
  444.5 0.8 copy.27
  (17 shorter events, 0.3 us)
Async XLA Ops:
  7.2 376.5 %copy-start = (f32[512,128]{1,0:T(8,128)S(1)}, f32[512,128]{1,0:T(8,128)}, u32[]{:S(2)}) copy-start(f32[512,128]{1,0:T(8,128)} %param.6) | copy-start | bytes 786436
  7.2 280.0 %all-gather.3.cloned.1.call-start = ((), (), s32[]{:S(2)}) async-start(), calls=%async_computation.1 | async-start | bytes 34603008 | tf_op jit(solution)/shard_map/all_gather | solution.py:12
  383.7 30.8 %copy-start.1 = (f32[512,512]{1,0:T(8,128)}, f32[512,512]{1,0:T(8,128)S(1)}, u32[]{:S(2)}) copy-start(f32[512,512]{1,0:T(8,128)S(1)} %select_select_fusion) | copy-start | bytes 3145732
Sparse Core Ops, SparseCore 0:
  92.4 194.7 all-gather.2
